TPU v7x, 32 devices: a whole 2x2x4 slice. The times are simulated.
32 devices in a mesh: dp: 4 (over y, x), ctx: 8 (over z, core).
Axes of the slice: x: 2, y: 2, z: 4, core: 2. Of those that a mesh axis runs over, the one named last changes fastest.
Arguments:
- inputs: float32 [4, 1024, 1088], P('dp', 'ctx'), may hold values from -6 to 6
- out_grad: float32 [4, 1024, 1088], P('dp', 'ctx'), may hold values from -6 to 6
- pair_blocks: int32 [8, 2], replicated, may hold values from 0 to 15, as said below
- triple_weight: float32 [1088, 3264], P('ctx', 'dp')
- merge_weight: float32 [1088, 1088], P('ctx', 'dp'), may hold values from -0.75 to 0.75
- expand_weight: float32 [1088, 4352], P('ctx', 'dp'), may hold values from -0.1875 to 0.1875
- shrink_weight: float32 [4352, 1088], P('ctx', 'dp'), may hold values from -0.09375 to 0.09375
- vector_params: float32 [1088, 12], P('ctx', 'dp')
- triple_moment: float32 [1088, 3264], P('ctx', 'dp'), may hold values from -24 to 24
- merge_moment: float32 [1088, 1088], P('ctx', 'dp'), may hold values from -6 to 6
- expand_moment: float32 [1088, 4352], P('ctx', 'dp'), may hold values from -6 to 6
- shrink_moment: float32 [4352, 1088], P('ctx', 'dp'), may hold values from -6 to 6
- vector_moment: float32 [1088, 12], P('ctx', 'dp'), may hold values from -112 to 112
- triple_square: float32 [1088, 3264], P('ctx', 'dp'), may hold values from 24.576 to 245.76
- merge_square: float32 [1088, 1088], P('ctx', 'dp'), may hold values from 8.192 to 81.92
- expand_square: float32 [1088, 4352], P('ctx', 'dp'), may hold values from 8.192 to 81.92
- shrink_square: float32 [4352, 1088], P('ctx', 'dp'), may hold values from 8.192 to 81.92
- vector_square: float32 [1088, 12], P('ctx', 'dp'), may hold values from 204.8 to 2048
Outputs:
- block_output: float32 [4, 1024, 1088], P('dp', 'ctx')
- input_grad: float32 [4, 1024, 1088], P('dp', 'ctx')
- triple_grad: float32 [1088, 3264], P('ctx', 'dp')
- merge_grad: float32 [1088, 1088], P('ctx', 'dp')
- expand_grad: float32 [1088, 4352], P('ctx', 'dp')
- shrink_grad: float32 [4352, 1088], P('ctx', 'dp')
- vector_grad: float32 [1088, 12], P('ctx', 'dp')
- triple_new: float32 [1088, 3264], P('ctx', 'dp')
- merge_new: float32 [1088, 1088], P('ctx', 'dp')
- expand_new: float32 [1088, 4352], P('ctx', 'dp')
- shrink_new: float32 [4352, 1088], P('ctx', 'dp')
- vector_new: float32 [1088, 12], P('ctx', 'dp')
- triple_moment_new: float32 [1088, 3264], P('ctx', 'dp')
- merge_moment_new: float32 [1088, 1088], P('ctx', 'dp')
- expand_moment_new: float32 [1088, 4352], P('ctx', 'dp')
- shrink_moment_new: float32 [4352, 1088], P('ctx', 'dp')
- vector_moment_new: float32 [1088, 12], P('ctx', 'dp')
- triple_square_new: float32 [1088, 3264], P('ctx', 'dp')
- merge_square_new: float32 [1088, 1088], P('ctx', 'dp')
- expand_square_new: float32 [1088, 4352], P('ctx', 'dp')
- shrink_square_new: float32 [4352, 1088], P('ctx', 'dp')
- vector_square_new: float32 [1088, 12], P('ctx', 'dp')
Inputs may be any that keep to these rules, and one draw needn't show every extreme that they name: `pair_blocks`: row c names the two blocks of 64 positions that stand in stored rows c * 2 * 64 onward: first a block p, then 2 * 8 - 1 - p; each of the 16 blocks is named once.
All inputs are finite; a program needn't handle non-finite values.
Results may differ from a plain program's by a relative error of at most 0.011.
Values may be sent and summed in bfloat16 or wider, within the bound.
A program may use at most 256 MiB of HBM per device.

v0:
```python
import jax
import jax.numpy as jnp
from jax import lax
from jax.sharding import PartitionSpec as P

D = 1088
H = 17
HD = 64
BLK = 64
norm_eps = 1e-05
beta_first = 0.9
beta_second = 0.95
learn_rate = 0.01
decay_rate = 0.1
adam_eps = 1e-08
adam_steps = 4
gelu_coef = 0.7978845608028654
masked_score = -1e30


def layer_norm(values):
    center = jnp.mean(values, axis=-1, keepdims=True)
    shifted = values - center
    inverse = lax.rsqrt(jnp.mean(shifted * shifted, axis=-1, keepdims=True) + norm_eps)
    return (shifted * inverse, inverse)


def norm_back(incoming, normed, inverse, gain_vec):
    scaled = incoming * gain_vec
    return inverse * (
        scaled
        - jnp.mean(scaled, axis=-1, keepdims=True)
        - normed * jnp.mean(scaled * normed, axis=-1, keepdims=True)
    )


def gelu_value(values):
    inside = gelu_coef * (values + 0.044715 * values * values * values)
    return 0.5 * values * (1.0 + jnp.tanh(inside))


def gelu_slope(values):
    inside = gelu_coef * (values + 0.044715 * values * values * values)
    tangent = jnp.tanh(inside)
    return 0.5 * (1.0 + tangent) + 0.5 * values * (1.0 - tangent * tangent) * gelu_coef * (
        1.0 + 3.0 * 0.044715 * values * values
    )


def adam_update(weight, gradient, moment, square, decayed):
    moment_new = beta_first * moment + (1.0 - beta_first) * gradient
    square_new = beta_second * square + (1.0 - beta_second) * gradient * gradient
    first_fix = 1.0 - beta_first**adam_steps
    second_fix = 1.0 - beta_second**adam_steps
    direction = moment_new / first_fix / (jnp.sqrt(square_new / second_fix) + adam_eps)
    if decayed:
        direction = direction + decay_rate * weight
    return (weight - learn_rate * direction, moment_new, square_new)


def split_heads(values):
    return values.reshape(values.shape[0], H, HD).transpose(1, 0, 2)


def join_heads(values):
    return values.transpose(1, 0, 2).reshape(values.shape[1], H * HD)


def gather_params(first_part, second_part, third_part, fourth_part, fifth_part):
    piece_one, piece_two, piece_three, piece_four, piece_five = (
        lax.all_gather(first_part, "ctx", axis=0, tiled=True),
        lax.all_gather(second_part, "ctx", axis=0, tiled=True),
        lax.all_gather(third_part, "ctx", axis=0, tiled=True),
        lax.all_gather(fourth_part, "ctx", axis=0, tiled=True),
        lax.all_gather(fifth_part, "ctx", axis=0, tiled=True),
    )
    return (
        lax.all_gather(piece_one, "dp", axis=1, tiled=True),
        lax.all_gather(piece_two, "dp", axis=1, tiled=True),
        lax.all_gather(piece_three, "dp", axis=1, tiled=True),
        lax.all_gather(piece_four, "dp", axis=1, tiled=True),
        lax.all_gather(piece_five, "dp", axis=1, tiled=True),
    )


def reduce_grads(first_part, second_part, third_part, fourth_part, fifth_part):
    piece_one, piece_two, piece_three, piece_four, piece_five = (
        lax.psum_scatter(first_part, "ctx", scatter_dimension=0, tiled=True),
        lax.psum_scatter(second_part, "ctx", scatter_dimension=0, tiled=True),
        lax.psum_scatter(third_part, "ctx", scatter_dimension=0, tiled=True),
        lax.psum_scatter(fourth_part, "ctx", scatter_dimension=0, tiled=True),
        lax.psum_scatter(fifth_part, "ctx", scatter_dimension=0, tiled=True),
    )
    return (
        lax.psum_scatter(piece_one, "dp", scatter_dimension=1, tiled=True),
        lax.psum_scatter(piece_two, "dp", scatter_dimension=1, tiled=True),
        lax.psum_scatter(piece_three, "dp", scatter_dimension=1, tiled=True),
        lax.psum_scatter(piece_four, "dp", scatter_dimension=1, tiled=True),
        lax.psum_scatter(piece_five, "dp", scatter_dimension=1, tiled=True),
    )


def gather_keys(key_rows, value_rows):
    return (
        lax.all_gather(key_rows, "ctx", axis=0, tiled=True),
        lax.all_gather(value_rows, "ctx", axis=0, tiled=True),
    )


def local(
    inputs,
    out_grad,
    pair_blocks,
    triple_weight,
    merge_weight,
    expand_weight,
    shrink_weight,
    vector_params,
    triple_moment,
    merge_moment,
    expand_moment,
    shrink_moment,
    vector_moment,
    triple_square,
    merge_square,
    expand_square,
    shrink_square,
    vector_square,
):
    rows_here = inputs.shape[1]
    stream = inputs[0]
    cotangent = out_grad[0]
    offsets = jnp.arange(BLK, dtype=jnp.int32)
    all_positions = (pair_blocks.reshape(-1)[:, None] * BLK + offsets[None, :]).reshape(-1)
    query_positions = lax.dynamic_slice_in_dim(
        all_positions, lax.axis_index("ctx") * rows_here, rows_here
    )
    allowed = query_positions[:, None] >= all_positions[None, :]
    score_scale = HD ** (-0.5)
    copy_triple = triple_weight.astype(jnp.bfloat16)
    copy_merge = merge_weight.astype(jnp.bfloat16)
    copy_expand = expand_weight.astype(jnp.bfloat16)
    copy_shrink = shrink_weight.astype(jnp.bfloat16)
    copy_vector = vector_params.astype(jnp.bfloat16)
    w_triple, w_merge, w_expand, w_shrink, w_vector = gather_params(
        copy_triple, copy_merge, copy_expand, copy_shrink, copy_vector
    )
    vectors = w_vector.astype(jnp.float32)
    gain_one = vectors[:, 0]
    shift_one = vectors[:, 1]
    query_bias = vectors[:, 2]
    value_bias = vectors[:, 3]
    merge_bias = vectors[:, 4]
    gain_two = vectors[:, 5]
    shift_two = vectors[:, 6]
    shrink_bias = vectors[:, 7]
    expand_bias = vectors[:, 8:12].T.reshape(-1)
    normed_one, inverse_one = layer_norm(stream)
    act_one = (normed_one * gain_one + shift_one).astype(jnp.bfloat16)
    triple = jnp.dot(act_one, w_triple, preferred_element_type=jnp.float32)
    query_b = (triple[:, :D] + query_bias).astype(jnp.bfloat16)
    key_b = triple[:, D : 2 * D].astype(jnp.bfloat16)
    value_b = (triple[:, 2 * D :] + value_bias).astype(jnp.bfloat16)
    keys_all, values_all = gather_keys(key_b, value_b)

    def head_scores(query_h, key_h):
        scores = (
            lax.dot_general(
                query_h, key_h, (((1,), (1,)), ((), ())), preferred_element_type=jnp.float32
            )
            * score_scale
        )
        return jnp.where(allowed, scores, masked_score)

    def head_forward(operands):
        query_h, key_h, value_h = operands
        scores = head_scores(query_h, key_h)
        row_max = jnp.max(scores, axis=1, keepdims=True)
        log_total = row_max + jnp.log(jnp.sum(jnp.exp(scores - row_max), axis=1, keepdims=True))
        probs_b = jnp.exp(scores - log_total).astype(jnp.bfloat16)
        attended = jnp.dot(probs_b, value_h, preferred_element_type=jnp.float32)
        return (attended.astype(jnp.bfloat16), log_total[:, 0])

    heads_query = split_heads(query_b)
    heads_key = split_heads(keys_all)
    heads_value = split_heads(values_all)
    heads_out, heads_total = lax.map(head_forward, (heads_query, heads_key, heads_value))
    attended_b = join_heads(heads_out)
    middle = stream + jnp.dot(attended_b, w_merge, preferred_element_type=jnp.float32) + merge_bias
    normed_two, inverse_two = layer_norm(middle)
    act_two = (normed_two * gain_two + shift_two).astype(jnp.bfloat16)
    pre_act = jnp.dot(act_two, w_expand, preferred_element_type=jnp.float32) + expand_bias
    hidden_b = gelu_value(pre_act).astype(jnp.bfloat16)
    block_out = (
        middle + jnp.dot(hidden_b, w_shrink, preferred_element_type=jnp.float32) + shrink_bias
    )
    back_triple, back_merge, back_expand, back_shrink, unused_vector = gather_params(
        copy_triple, copy_merge, copy_expand, copy_shrink, copy_vector
    )
    keys_again, values_again = gather_keys(key_b, value_b)
    back_key = split_heads(keys_again)
    back_value = split_heads(values_again)
    cotangent_b = cotangent.astype(jnp.bfloat16)
    shrink_local = jnp.dot(hidden_b.T, cotangent_b, preferred_element_type=jnp.float32)
    shrink_bias_grad = jnp.sum(cotangent, axis=0)
    dpre = jnp.dot(cotangent_b, back_shrink.T, preferred_element_type=jnp.float32) * gelu_slope(
        pre_act
    )
    dpre_b = dpre.astype(jnp.bfloat16)
    expand_local = jnp.dot(act_two.T, dpre_b, preferred_element_type=jnp.float32)
    expand_bias_grad = jnp.sum(dpre, axis=0)
    dact_two = jnp.dot(dpre_b, back_expand.T, preferred_element_type=jnp.float32)
    gain_two_grad = jnp.sum(dact_two * normed_two, axis=0)
    shift_two_grad = jnp.sum(dact_two, axis=0)
    dmiddle = cotangent + norm_back(dact_two, normed_two, inverse_two, gain_two)
    dmiddle_b = dmiddle.astype(jnp.bfloat16)
    merge_local = jnp.dot(attended_b.T, dmiddle_b, preferred_element_type=jnp.float32)
    merge_bias_grad = jnp.sum(dmiddle, axis=0)
    dattended_b = jnp.dot(dmiddle_b, back_merge.T, preferred_element_type=jnp.float32).astype(
        jnp.bfloat16
    )

    def head_backward(operands):
        query_h, key_h, value_h, out_h, dout_h, log_total = operands
        scores = head_scores(query_h, key_h)
        probs = jnp.exp(scores - log_total[:, None])
        probs_b = probs.astype(jnp.bfloat16)
        delta = jnp.sum(
            dout_h.astype(jnp.float32) * out_h.astype(jnp.float32), axis=1, keepdims=True
        )
        dprobs = lax.dot_general(
            dout_h, value_h, (((1,), (1,)), ((), ())), preferred_element_type=jnp.float32
        )
        dscores_b = (probs * (dprobs - delta) * score_scale).astype(jnp.bfloat16)
        dquery_h = jnp.dot(dscores_b, key_h, preferred_element_type=jnp.float32)
        dkey_h = lax.dot_general(
            dscores_b, query_h, (((0,), (0,)), ((), ())), preferred_element_type=jnp.float32
        )
        dvalue_h = lax.dot_general(
            probs_b, dout_h, (((0,), (0,)), ((), ())), preferred_element_type=jnp.float32
        )
        return (dquery_h, dkey_h, dvalue_h)

    dquery_heads, dkey_heads, dvalue_heads = lax.map(
        head_backward,
        (heads_query, back_key, back_value, heads_out, split_heads(dattended_b), heads_total),
    )
    dquery = join_heads(dquery_heads)
    dkey_rows, dvalue_rows = (
        lax.psum_scatter(join_heads(dkey_heads), "ctx", scatter_dimension=0, tiled=True),
        lax.psum_scatter(join_heads(dvalue_heads), "ctx", scatter_dimension=0, tiled=True),
    )
    dtriple_b = jnp.concatenate([dquery, dkey_rows, dvalue_rows], axis=1).astype(jnp.bfloat16)
    triple_local = jnp.dot(act_one.T, dtriple_b, preferred_element_type=jnp.float32)
    query_bias_grad = jnp.sum(dquery, axis=0)
    value_bias_grad = jnp.sum(dvalue_rows, axis=0)
    dact_one = jnp.dot(dtriple_b, back_triple.T, preferred_element_type=jnp.float32)
    gain_one_grad = jnp.sum(dact_one * normed_one, axis=0)
    shift_one_grad = jnp.sum(dact_one, axis=0)
    input_rows = dmiddle + norm_back(dact_one, normed_one, inverse_one, gain_one)
    vector_local = jnp.concatenate(
        [
            jnp.stack(
                [
                    gain_one_grad,
                    shift_one_grad,
                    query_bias_grad,
                    value_bias_grad,
                    merge_bias_grad,
                    gain_two_grad,
                    shift_two_grad,
                    shrink_bias_grad,
                ],
                axis=1,
            ),
            expand_bias_grad.reshape(4, D).T,
        ],
        axis=1,
    )
    triple_grad, merge_grad, expand_grad, shrink_grad, vector_grad = reduce_grads(
        triple_local, merge_local, expand_local, shrink_local, vector_local
    )
    triple_new, triple_moment_new, triple_square_new = adam_update(
        triple_weight, triple_grad, triple_moment, triple_square, True
    )
    merge_new, merge_moment_new, merge_square_new = adam_update(
        merge_weight, merge_grad, merge_moment, merge_square, True
    )
    expand_new, expand_moment_new, expand_square_new = adam_update(
        expand_weight, expand_grad, expand_moment, expand_square, True
    )
    shrink_new, shrink_moment_new, shrink_square_new = adam_update(
        shrink_weight, shrink_grad, shrink_moment, shrink_square, True
    )
    vector_new, vector_moment_new, vector_square_new = adam_update(
        vector_params, vector_grad, vector_moment, vector_square, False
    )
    return (
        block_out[None],
        input_rows[None],
        triple_grad,
        merge_grad,
        expand_grad,
        shrink_grad,
        vector_grad,
        triple_new,
        merge_new,
        expand_new,
        shrink_new,
        vector_new,
        triple_moment_new,
        merge_moment_new,
        expand_moment_new,
        shrink_moment_new,
        vector_moment_new,
        triple_square_new,
        merge_square_new,
        expand_square_new,
        shrink_square_new,
        vector_square_new,
    )


def solution(mesh):
    in_specs = (
        P("dp", "ctx", None),
        P("dp", "ctx", None),
        P(),
        P("ctx", "dp"),
        P("ctx", "dp"),
        P("ctx", "dp"),
        P("ctx", "dp"),
        P("ctx", "dp"),
        P("ctx", "dp"),
        P("ctx", "dp"),
        P("ctx", "dp"),
        P("ctx", "dp"),
        P("ctx", "dp"),
        P("ctx", "dp"),
        P("ctx", "dp"),
        P("ctx", "dp"),
        P("ctx", "dp"),
        P("ctx", "dp"),
    )
    out_specs = (
        P("dp", "ctx", None),
        P("dp", "ctx", None),
        P("ctx", "dp"),
        P("ctx", "dp"),
        P("ctx", "dp"),
        P("ctx", "dp"),
        P("ctx", "dp"),
        P("ctx", "dp"),
        P("ctx", "dp"),
        P("ctx", "dp"),
        P("ctx", "dp"),
        P("ctx", "dp"),
        P("ctx", "dp"),
        P("ctx", "dp"),
        P("ctx", "dp"),
        P("ctx", "dp"),
        P("ctx", "dp"),
        P("ctx", "dp"),
        P("ctx", "dp"),
        P("ctx", "dp"),
        P("ctx", "dp"),
        P("ctx", "dp"),
    )
    return jax.shard_map(local, mesh=mesh, in_specs=in_specs, out_specs=out_specs, check_vma=False)
```

profile of v0, /device:TPU:0, one launch (start us, length us, event | category | flops | bytes accessed | tf_op | source)
XLA Modules:
  0.0 1586.2 jit_solution(11072138455714467575)
XLA Ops:
  9.1 31.8 %all-gather.13.cloned.1.call-done = bf16[1088,816]{1,0:T(8,128)(2,1)} async-done(((bf16[136,816]{1,0:T(8,128)(2,1)}), bf16[1088,816]{1,0:T(8,128)(2,1)}) %all-gather.13.cloned.1.call-update) | async-done | bytes 1775632 | tf_op jit(solution)/shard_map/all_gather | solution.py:71
  40.9 4.0 copy.90
  46.9 12.8 all-gather
  59.8 8.8 all-gather.1
  69.6 55.4 %all-gather.15.cloned.1.call-done = bf16[1088,3264]{0,1:T(8,128)(2,1)} async-done(((bf16[1088,816]{0,1:T(8,128)(2,1)}), bf16[1088,3264]{0,1:T(8,128)(2,1)}) %all-gather.15.cloned.1.call-update) | async-done | bytes 7102480 | tf_op jit(solution)/shard_map/all_gather | solution.py:78
  125.0 5.4 fusion.75
  132.6 21.3 %all_gather.52 = bf16[1088,272]{1,0:T(8,128)(2,1)S(1)} all-gather(bf16[136,272]{1,0:T(8,128)(2,1)S(1)} %convert_element_type.74), channel_id=1, replica_groups=mesh['dp'=4,'ctx'=8] {'ctx'}, dimensions={0}, use_global_device_ids=true | all-gather | bytes 665856 | tf_op jit(solution)/shard_map/all_gather | solution.py:72
  155.0 11.0 all-gather.23.cloned.1.call-done
  166.0 5.1 copy.96
  173.4 28.5 %all-gather.29.cloned.1.call-done = bf16[8,544,272]{1,2,0:T(8,128)(2,1)} async-done(((bf16[1,544,272]{1,2,0:T(8,128)(2,1)}), bf16[8,544,272]{1,2,0:T(8,128)(2,1)}) %all-gather.29.cloned.1.call-update) | async-done | bytes 2367504 | tf_op jit(solution)/shard_map/all_gather | solution.py:74
  204.3 3.1 reshape.198
  208.6 26.0 %all-gather.17.cloned.1.call-done = bf16[1024,1088]{0,1:T(8,128)(2,1)} async-done(((bf16[128,1088]{0,1:T(8,128)(2,1)}), bf16[1024,1088]{0,1:T(8,128)(2,1)}) %all-gather.17.cloned.1.call-update) | async-done | bytes 2228240 | tf_op jit(solution)/shard_map/all_gather | solution.py:105
  234.7 5.2 copy.92
  239.9 27.4 %all-gather.19.cloned.1.call-done = bf16[1024,1088]{0,1:T(8,128)(2,1)} async-done(((bf16[128,1088]{0,1:T(8,128)(2,1)}), bf16[1024,1088]{0,1:T(8,128)(2,1)}) %all-gather.19.cloned.1.call-update) | async-done | bytes 2228240 | tf_op jit(solution)/shard_map/all_gather | solution.py:106
  267.3 5.3 copy.93
  272.6 69.9 %while.28 = (s32[]{:T(128)}, bf16[17,128,64]{1,2,0:T(8,128)(2,1)S(1)}, f32[17,128]{1,0:T(8,128)}, bf16[17,128,64]{2,1,0:T(8,128)(2,1)S(1)}, bf16[17,1024,64]{2,1...) while((s32[]{:T(128)}, ...), condition=%wide.region_5.6_spmd.clone, body=%wide.region_2.5_spmd.clone.sunk | while | flops 34611072 | bytes 2157681 | solution.py:187
  343.3 2.5 fusion.86
  346.6 63.8 %all-gather.25.cloned.1.call-done = bf16[1088,4352]{0,1:T(8,128)(2,1)} async-done(((bf16[1088,1088]{0,1:T(8,128)(2,1)}), bf16[1088,4352]{0,1:T(8,128)(2,1)}) %all-gather.25.cloned.1.call-update) | async-done | bytes 9469968 | tf_op jit(solution)/shard_map/all_gather | solution.py:80
  410.4 7.3 convolution_add_fusion
  417.6 91.1 %all-gather.27.cloned.1.call-done = bf16[4352,1088]{0,1:T(8,128)(2,1)} async-done(((bf16[4352,272]{0,1:T(8,128)(2,1)}), bf16[4352,1088]{0,1:T(8,128)(2,1)}) %all-gather.27.cloned.1.call-update) | async-done | bytes 9469968 | tf_op jit(solution)/shard_map/all_gather | solution.py:81
  508.8 7.5 fusion.87
  516.3 4.9 multiply_reduce_fusion
  523.8 133.4 %while.29 = (s32[]{:T(128)}, f32[17,128,64]{1,2,0:T(8,128)}, f32[17,1024,64]{1,2,0:T(8,128)}, f32[17,1024,64]{1,2,0:T(8,128)}, bf16[17,128,64]{2,1,0:T(8,128)(2,...) while((s32[]{:T(128)}, f32[17,128,64]{1,2,0:T(8,128)}, ...), condition=%wide.region_12.13_spmd.clone, body=%wide.region_10.12_spmd.clone.sunk | while | flops 85098368 | bytes 3944593 | solution.py:244
  658.1 3.0 fusion.69
  662.7 9.6 fusion.68
  674.2 35.6 %reduce-scatter.20.cloned.1.call-done = f32[128,1088]{0,1:T(8,128)} async-done(((f32[1024,1088]{0,1:T(8,128)}), f32[128,1088]{0,1:T(8,128)}) %reduce-scatter.20.cloned.1.call-update) | async-done | bytes 557072 | tf_op jit(solution)/shard_map/reduce_scatter | solution.py:250
  711.6 51.4 %reduce-scatter.22.cloned.1.call-done = f32[128,1088]{0,1:T(8,128)} async-done(((f32[1024,1088]{0,1:T(8,128)}), f32[128,1088]{0,1:T(8,128)}) %reduce-scatter.22.cloned.1.call-update) | async-done | bytes 557072 | tf_op jit(solution)/shard_map/reduce_scatter | solution.py:251
  765.8 8.5 fusion.65
  774.9 9.5 fusion.59
  784.5 37.1 %reduce-scatter.36.cloned.1.call-done = f32[136,1088]{1,0:T(8,128)} async-done(((f32[1088,1088]{1,0:T(8,128)}), f32[136,1088]{1,0:T(8,128)}) %reduce-scatter.36.cloned.1.call-update) | async-done | bytes 591888
  821.6 2.4 copy.110
  824.1 197.3 %reduce-scatter.28.cloned.1.call-done = f32[544,1088]{1,0:T(8,128)} async-done(((f32[4352,1088]{1,0:T(8,128)}), f32[544,1088]{1,0:T(8,128)}) %reduce-scatter.28.cloned.1.call-update) | async-done | bytes 2367504 | tf_op jit(solution)/shard_map/reduce_scatter | solution.py:91
  1021.5 147.7 %reduce-scatter.24.cloned.1.call-done = f32[136,3264]{1,0:T(8,128)} async-done(((f32[1088,3264]{1,0:T(8,128)}), f32[136,3264]{1,0:T(8,128)}) %reduce-scatter.24.cloned.1.call-update) | async-done | bytes 1775632 | tf_op jit(solution)/shard_map/reduce_scatter | solution.py:88
  1169.2 3.4 copy.108
  1172.7 186.2 %reduce-scatter.26.cloned.1.call-done = f32[136,4352]{1,0:T(8,128)} async-done(((f32[1088,4352]{1,0:T(8,128)}), f32[136,4352]{1,0:T(8,128)}) %reduce-scatter.26.cloned.1.call-update) | async-done | bytes 2367504 | tf_op jit(solution)/shard_map/reduce_scatter | solution.py:90
  1358.9 5.0 copy.112
  1370.5 2.4 copy.101
  1386.5 7.3 fusion.49
  1394.0 7.2 multiply_reduce_fusion.1
  1402.6 28.0 %all-reduce.2 = f32[1088,12]{0,1:T(8,128)} all-reduce(f32[1088,12]{0,1:T(8,128)} %concatenate.8), channel_id=12, replica_groups=mesh['dp'=4,'ctx'=8] {'ctx'}, use_global_device_ids=true, to_apply=%region_34.35.clone | all-reduce | flops 13056 | bytes 104448
  1432.0 17.5 %all-reduce.3 = f32[136,12]{0,1:T(8,128)} all-reduce(f32[136,12]{0,1:T(8,128)} %constant_dynamic-slice_fusion.2), channel_id=13, replica_groups=mesh['dp'=4,'ctx'=8] {'dp'}, use_global_device_ids=true, to_apply=%region_35.36.clone | all-reduce | flops 1632 | bytes 13056
  1457.1 11.4 all-reduce.6.cloned.1.call-done
  1468.5 3.9 multiply_subtract_fusion
  1472.4 2.4 copy.104
  1479.5 37.7 %reduce-scatter.30.cloned.1.call-done = f32[816,136]{1,0:T(8,128)} async-done(((f32[3264,136]{1,0:T(8,128)}), f32[816,136]{1,0:T(8,128)}) %reduce-scatter.30.cloned.1.call-update) | async-done | bytes 443920
  1518.6 2.7 multiply_subtract_fusion.2
  1521.3 53.7 %reduce-scatter.34.cloned.1.call-done = f32[1088,136]{1,0:T(8,128)} async-done(((f32[4352,136]{1,0:T(8,128)}), f32[1088,136]{1,0:T(8,128)}) %reduce-scatter.34.cloned.1.call-update) | async-done | bytes 591888
  1576.6 2.9 multiply_subtract_fusion.1
  (461 shorter events, 266.3 us)
Async XLA Ops:
  7.2 33.7 %all-gather.13.cloned.1.call-start = ((), (), s32[]{:S(2)}) async-start(), calls=%async_computation.9 | async-start | bytes 2193408 | tf_op jit(solution)/shard_map/all_gather | solution.py:71
  9.0 35.9 %copy-start.14 = (f32[136,1088]{1,0:T(8,128)S(1)}, f32[136,1088]{1,0:T(8,128)}, u32[]{:S(2)}) copy-start(f32[136,1088]{1,0:T(8,128)} %param.27) | copy-start | bytes 1775620
  9.0 116.0 %all-gather.15.cloned.1.call-start = ((), (), s32[]{:S(2)}) async-start(), calls=%async_computation.10 | async-start | bytes 9400320 | tf_op jit(solution)/shard_map/all_gather | solution.py:78
  44.9 23.7 %copy-start.1 = (f32[1,128,1088]{1,2,0:T(8,128)S(1)}, f32[1,128,1088]{1,2,0:T(8,128)}, u32[]{:S(2)}) copy-start(f32[1,128,1088]{1,2,0:T(8,128)} %param.22) | copy-start | bytes 1671172
  44.9 121.1 %all-gather.23.cloned.1.call-start = ((), (), s32[]{:S(2)}) async-start(), calls=%async_computation.14 | async-start | bytes 2820096 | tf_op jit(solution)/shard_map/all_gather | solution.py:73
  45.7 156.2 %all-gather.29.cloned.1.call-start = ((), (), s32[]{:S(2)}) async-start(), calls=%async_computation.22 | async-start | bytes 3133440 | tf_op jit(solution)/shard_map/all_gather | solution.py:74
  46.9 187.8 %all-gather.17.cloned.1.call-start = ((), (), s32[]{:S(2)}) async-start(), calls=%async_computation.11 | async-start | bytes 2506752 | tf_op jit(solution)/shard_map/all_gather | solution.py:105
  69.4 61.0 %copy-start.32 = (f32[1088]{0:T(1024)}, f32[1088]{0:T(1024)S(1)}, u32[]{:S(2)}) copy-start(f32[1088]{0:T(1024)S(1)} %get-tuple-element.323) | copy-start | bytes 13060
  69.4 61.0 %copy-start.34 = (f32[1088]{0:T(1024)}, f32[1088]{0:T(1024)S(1)}, u32[]{:S(2)}) copy-start(f32[1088]{0:T(1024)S(1)} %get-tuple-element.322) | copy-start | bytes 13060
  69.5 61.0 %copy-start.47 = (f32[128]{0:T(128)}, f32[128]{0:T(128)S(1)}, u32[]{:S(2)}) copy-start(f32[128]{0:T(128)S(1)} %broadcast_multiply_fusion.6) | copy-start | bytes 1540
  69.6 60.8 %copy-start.51 = (f32[128]{0:T(128)}, f32[128]{0:T(128)S(1)}, u32[]{:S(2)}) copy-start(f32[128]{0:T(128)S(1)} %add_rsqrt_fusion.1) | copy-start | bytes 1540
  131.2 136.1 %all-gather.19.cloned.1.call-start = ((), (), s32[]{:S(2)}) async-start(), calls=%async_computation.12 | async-start | bytes 2506752 | tf_op jit(solution)/shard_map/all_gather | solution.py:106
  132.5 210.1 %all-gather.21.cloned.1.call-start = ((), (), s32[]{:S(2)}) async-start(), calls=%async_computation.13 | async-start | bytes 3133440 | tf_op jit(solution)/shard_map/all_gather | solution.py:79
  155.0 255.4 %all-gather.25.cloned.1.call-start = ((), (), s32[]{:S(2)}) async-start(), calls=%async_computation.15 | async-start | bytes 12533760 | tf_op jit(solution)/shard_map/all_gather | solution.py:80
  171.2 337.6 %all-gather.27.cloned.1.call-start = ((), (), s32[]{:S(2)}) async-start(), calls=%async_computation.16 | async-start | bytes 11837440 | tf_op jit(solution)/shard_map/all_gather | solution.py:81
  207.4 502.4 %reduce-scatter.20.cloned.1.call-start = ((), (), s32[]{:S(2)}) async-start(), calls=%async_computation.17 | async-start | bytes 5013504 | tf_op jit(solution)/shard_map/reduce_scatter | solution.py:250
  272.6 70.7 %copy-start.37 = (f32[1088]{0:T(1024)S(1)}, f32[1088]{0:T(1024)}, u32[]{:S(2)}) copy-start(f32[1088]{0:T(1024)} %get-tuple-element.319) | copy-start | bytes 13060
  345.9 64.5 %copy-start.38 = (f32[128]{0:T(128)}, f32[128]{0:T(128)S(1)}, u32[]{:S(2)}) copy-start(f32[128]{0:T(128)S(1)} %broadcast_multiply_fusion.5) | copy-start | bytes 1540
  417.6 98.6 %copy-start.3 = (f32[128,4352]{1,0:T(8,128)}, f32[128,4352]{1,0:T(8,128)S(1)}, u32[]{:S(2)}) copy-start(f32[128,4352]{1,0:T(8,128)S(1)} %convolution_add_fusion) | copy-start | bytes 6684676
  508.7 7.5 copy-start
  508.7 7.5 copy-start.31
  508.7 7.5 copy-start.39
  508.7 7.5 copy-start.41
  522.2 135.8 %copy-start.5 = (f32[128,1088]{0,1:T(8,128)}, f32[128,1088]{0,1:T(8,128)S(1)}, u32[]{:S(2)}) copy-start(f32[128,1088]{0,1:T(8,128)S(1)} %get-tuple-element.382) | copy-start | bytes 1671172
  657.3 105.8 %reduce-scatter.22.cloned.1.call-start = ((), (), s32[]{:S(2)}) async-start(), calls=%async_computation.18 | async-start | bytes 5013504 | tf_op jit(solution)/shard_map/reduce_scatter | solution.py:251
  658.0 163.6 %reduce-scatter.36.cloned.1.call-start = ((), (), s32[]{:S(2)}) async-start(), calls=%async_computation.27 | async-start | bytes 5640192
  661.1 360.4 %reduce-scatter.28.cloned.1.call-start = ((), (), s32[]{:S(2)}) async-start(), calls=%async_computation.21 | async-start | bytes 22560768 | tf_op jit(solution)/shard_map/reduce_scatter | solution.py:91
  672.3 93.5 %copy-start.48 = (f32[128]{0:T(128)S(1)}, f32[128]{0:T(128)}, u32[]{:S(2)}) copy-start(f32[128]{0:T(128)} %copy-done.47) | copy-start | bytes 1540
  672.3 496.9 %reduce-scatter.24.cloned.1.call-start = ((), (), s32[]{:S(2)}) async-start(), calls=%async_computation.19 | async-start | bytes 16293888 | tf_op jit(solution)/shard_map/reduce_scatter | solution.py:88
  774.3 584.6 %reduce-scatter.26.cloned.1.call-start = ((), (), s32[]{:S(2)}) async-start(), calls=%async_computation.20 | async-start | bytes 21307392 | tf_op jit(solution)/shard_map/reduce_scatter | solution.py:90
  784.5 669.4 %reduce-scatter.32.cloned.1.call-start = ((), (), s32[]{:S(2)}) async-start(), calls=%async_computation.24 | async-start | bytes 1392640
  824.1 644.4 %all-reduce.6.cloned.1.call-start = ((), (), s32[]{:S(2)}) async-start(), calls=%async_computation.26 | async-start | bytes 5013504
  1021.5 495.7 %reduce-scatter.30.cloned.1.call-start = ((), (), s32[]{:S(2)}) async-start(), calls=%async_computation.23 | async-start | bytes 4177920
  1172.7 402.3 %reduce-scatter.34.cloned.1.call-start = ((), (), s32[]{:S(2)}) async-start(), calls=%async_computation.25 | async-start | bytes 5570560
  1363.9 11.5 copy-start.56
  1386.5 7.4 copy-start.25
  1386.5 7.4 copy-start.27
  1386.5 7.4 copy-start.33
  1386.5 7.4 copy-start.49
  1386.5 7.4 copy-start.52
  1394.0 58.2 %copy-start.6 = (f32[128,1088]{0,1:T(8,128)S(1)}, f32[128,1088]{0,1:T(8,128)}, u32[]{:S(2)}) copy-start(f32[128,1088]{0,1:T(8,128)} %copy-done.5) | copy-start | bytes 1671172
  1402.6 66.0 %copy-start.9 = (f32[544,272]{1,0:T(8,128)S(1)}, f32[544,272]{1,0:T(8,128)}, u32[]{:S(2)}) copy-start(f32[544,272]{1,0:T(8,128)} %copy.103) | copy-start | bytes 1775620
  1402.6 66.0 %copy-start.10 = (f32[544,272]{1,0:T(8,128)S(1)}, f32[544,272]{1,0:T(8,128)}, u32[]{:S(2)}) copy-start(f32[544,272]{1,0:T(8,128)} %copy.100) | copy-start | bytes 1775620
  1455.0 17.4 %copy-start.29 = (f32[136,272]{1,0:T(8,128)}, f32[136,272]{1,0:T(8,128)S(1)}, u32[]{:S(2)}) copy-start(f32[136,272]{1,0:T(8,128)S(1)} %copy.111) | copy-start | bytes 443908
  1477.1 41.4 %copy-start.18 = (f32[136,816]{1,0:T(8,128)S(1)}, f32[136,816]{1,0:T(8,128)}, u32[]{:S(2)}) copy-start(f32[136,816]{1,0:T(8,128)} %param.25) | copy-start | bytes 1331716
  1518.6 58.0 %copy-start.17 = (f32[136,816]{1,0:T(8,128)}, f32[136,816]{1,0:T(8,128)S(1)}, u32[]{:S(2)}) copy-start(f32[136,816]{1,0:T(8,128)S(1)} %copy.109) | copy-start | bytes 1331716
  1518.6 58.0 %copy-start.15 = (f32[136,1088]{1,0:T(8,128)S(1)}, f32[136,1088]{1,0:T(8,128)}, u32[]{:S(2)}) copy-start(f32[136,1088]{1,0:T(8,128)} %param.27) | copy-start | bytes 1775620
  1518.6 58.0 %copy-start.30 = (f32[136,1088]{1,0:T(8,128)S(1)}, f32[136,1088]{1,0:T(8,128)}, u32[]{:S(2)}) copy-start(f32[136,1088]{1,0:T(8,128)} %param.32) | copy-start | bytes 1775620
  (28 other events, 115.5 us)
Sparse Core Ops, SparseCore 0:
  10.2 30.6 all-gather.12
  45.0 79.9 all-gather.14
  127.2 38.7 all-gather.22
  168.1 33.8 all-gather.28
  203.9 30.6 all-gather.16
  236.7 30.5 all-gather.18
  269.7 37.5 all-gather.20
  309.2 101.1 all-gather.24
  412.2 96.4 all-gather.26
  657.4 52.3 reduce-scatter.19
  712.1 50.8 reduce-scatter.21
  765.2 56.3 reduce-scatter.35
  824.0 197.4 reduce-scatter.27
  1023.6 145.5 reduce-scatter.23
  1171.4 187.4 reduce-scatter.25
  1361.7 26.8 reduce-scatter.31
  1391.6 76.8 all-reduce.5
  1471.4 45.6 reduce-scatter.29
  1520.2 54.7 reduce-scatter.33
where the time goes:
time: 1600 us; the launch traced here: 1590 us
  waiting for transfers between devices  1090 us (68%)
  matrix products  234 us (15%)
  local copies, waits for them, and re-layouts  113 us (7%)
  blocking collectives  88.3 us (6%)
  other arithmetic  38.1 us (2%)
  between operations  16.8 us (1%)
    reduce_scatter x1, waiting for transfers between devices, reduce_grads(): lax.psum_scatter(fourth_part, 'ctx', scatter_dimension=0, tiled=True)  197 us
    reduce_scatter x1, waiting for transfers between devices, reduce_grads(): lax.psum_scatter(third_part, 'ctx', scatter_dimension=0, tiled=True)  186 us
    reduce_scatter x1, waiting for transfers between devices, reduce_grads(): lax.psum_scatter(first_part, 'ctx', scatter_dimension=0, tiled=True)  148 us
    unnamed x24, waiting for transfers between devices  141 us
    all_gather x1, waiting for transfers between devices, gather_params(): lax.all_gather(piece_four, 'dp', axis=1, tiled=True)  91.1 us
    all_gather x1, waiting for transfers between devices, gather_params(): lax.all_gather(piece_three, 'dp', axis=1, tiled=True)  63.8 us
    all_gather x1, waiting for transfers between devices, gather_params(): lax.all_gather(piece_one, 'dp', axis=1, tiled=True)  55.4 us
    reduce_scatter x1, waiting for transfers between devices, local(): lax.psum_scatter(join_heads(dvalue_heads), 'ctx', scatter_dimension=0, ti...  51.4 us
  transfers between devices with their start and end apart: 19, of which 17 were waited for; matrix products, arithmetic and copies ran while one was open for 14% of the time, Pallas kernels for 0%

commit v1 on v0

--- a/solution.py
+++ b/solution.py
@@ -78,7 +78,9 @@
         lax.all_gather(piece_one, "dp", axis=1, tiled=True),
         lax.all_gather(piece_two, "dp", axis=1, tiled=True),
         lax.all_gather(piece_three, "dp", axis=1, tiled=True),
-        lax.all_gather(piece_four, "dp", axis=1, tiled=True),
+        jnp.concatenate(
+            lax.all_to_all(jnp.stack([piece_four] * lax.axis_size("dp")), "dp", 0, 0), axis=1
+        ),
         lax.all_gather(piece_five, "dp", axis=1, tiled=True),
     )
 

time: 1600 us -> 1520 us (0.950)
  waiting for transfers between devices: 1090 us -> 1000 us
    all_gather x1 -> x0, waiting for transfers between devices: 91.1 us -> none  [gather_params(): lax.all_gather(piece_four, 'dp', axis=1, tiled=True)]
    all_gather x1, waiting for transfers between devices: 28.5 us -> 11.6 us  [gather_params(): lax.all_gather(fourth_part, 'ctx', axis=0, tiled=True)]
    unnamed x24 -> x23, waiting for transfers between devices: 141 us -> 141 us
  transfers between devices with their start and end apart: 19 -> 19, of which waited for: 17 -> 16; matrix products, arithmetic and copies ran while one was open for 14% -> 15% of each run, Pallas kernels for 0% -> 0%
where the time goes in v1:
time: 1520 us; the launch traced here: 1510 us
  waiting for transfers between devices  1000 us (66%)
  matrix products  235 us (15%)
  local copies, waits for them, and re-layouts  118 us (8%)
  blocking collectives  88.3 us (6%)
  other arithmetic  38.1 us (3%)
  between operations  17.2 us (1%)
    reduce_scatter x1, waiting for transfers between devices, reduce_grads(): lax.psum_scatter(fourth_part, 'ctx', scatter_dimension=0, tiled=True)  197 us
    reduce_scatter x1, waiting for transfers between devices, reduce_grads(): lax.psum_scatter(third_part, 'ctx', scatter_dimension=0, tiled=True)  186 us
    reduce_scatter x1, waiting for transfers between devices, reduce_grads(): lax.psum_scatter(first_part, 'ctx', scatter_dimension=0, tiled=True)  148 us
    unnamed x23, waiting for transfers between devices  141 us
    all_gather x1, waiting for transfers between devices, gather_params(): lax.all_gather(piece_three, 'dp', axis=1, tiled=True)  73.3 us
    all_gather x1, waiting for transfers between devices, gather_params(): lax.all_gather(piece_one, 'dp', axis=1, tiled=True)  55.4 us
    reduce_scatter x1, waiting for transfers between devices, local(): lax.psum_scatter(join_heads(dvalue_heads), 'ctx', scatter_dimension=0, ti...  51.3 us
    unnamed x2, blocking collectives  45.5 us
  transfers between devices with their start and end apart: 19, of which 16 were waited for; matrix products, arithmetic and copies ran while one was open for 15% of the time, Pallas kernels for 0%

profile of v1, /device:TPU:0, one launch (start us, length us, event | category | flops | bytes accessed | tf_op | source)
XLA Modules:
  0.0 1505.2 jit_solution(719009018444153431)
XLA Ops:
  9.1 31.8 %all-gather.12.cloned.1.call-done = bf16[1088,816]{1,0:T(8,128)(2,1)} async-done(((bf16[136,816]{1,0:T(8,128)(2,1)}), bf16[1088,816]{1,0:T(8,128)(2,1)}) %all-gather.12.cloned.1.call-update) | async-done | bytes 1775632 | tf_op jit(solution)/shard_map/all_gather | solution.py:71
  40.9 3.9 copy.90
  46.9 12.8 all-gather
  59.7 8.8 all-gather.1
  69.6 55.4 %all-gather.14.cloned.1.call-done = bf16[1088,3264]{0,1:T(8,128)(2,1)} async-done(((bf16[1088,816]{0,1:T(8,128)(2,1)}), bf16[1088,3264]{0,1:T(8,128)(2,1)}) %all-gather.14.cloned.1.call-update) | async-done | bytes 7102480 | tf_op jit(solution)/shard_map/all_gather | solution.py:78
  125.0 5.4 fusion.77
  132.5 21.2 %all_gather.48 = bf16[1088,272]{1,0:T(8,128)(2,1)S(1)} all-gather(bf16[136,272]{1,0:T(8,128)(2,1)S(1)} %convert_element_type.79), channel_id=1, replica_groups=mesh['dp'=4,'ctx'=8] {'ctx'}, dimensions={0}, use_global_device_ids=true | all-gather | bytes 665856 | tf_op jit(solution)/shard_map/all_gather | solution.py:72
  156.6 11.6 all-gather.26.cloned.1.call-done
  170.6 3.0 reshape.211
  173.6 5.9 stack.36
  179.6 5.8 all-to-all-start
  185.4 16.3 %all-gather.22.cloned.1.call-done = bf16[1088,1088]{1,0:T(8,128)(2,1)} async-done(((bf16[136,1088]{1,0:T(8,128)(2,1)}), bf16[1088,1088]{1,0:T(8,128)(2,1)}) %all-gather.22.cloned.1.call-update) | async-done | bytes 2367504 | tf_op jit(solution)/shard_map/all_gather | solution.py:73
  201.7 5.1 copy.96
  208.2 26.4 %all-gather.16.cloned.1.call-done = bf16[1024,1088]{0,1:T(8,128)(2,1)} async-done(((bf16[128,1088]{0,1:T(8,128)(2,1)}), bf16[1024,1088]{0,1:T(8,128)(2,1)}) %all-gather.16.cloned.1.call-update) | async-done | bytes 2228240 | tf_op jit(solution)/shard_map/all_gather | solution.py:107
  234.6 5.2 copy.92
  239.8 27.1 %all-gather.18.cloned.1.call-done = bf16[1024,1088]{0,1:T(8,128)(2,1)} async-done(((bf16[128,1088]{0,1:T(8,128)(2,1)}), bf16[1024,1088]{0,1:T(8,128)(2,1)}) %all-gather.18.cloned.1.call-update) | async-done | bytes 2228240 | tf_op jit(solution)/shard_map/all_gather | solution.py:108
  267.0 5.3 copy.93
  272.2 69.9 %while.28 = (s32[]{:T(128)}, bf16[17,128,64]{1,2,0:T(8,128)(2,1)S(1)}, f32[17,128]{1,0:T(8,128)}, bf16[17,128,64]{2,1,0:T(8,128)(2,1)S(1)}, bf16[17,1024,64]{2,1...) while((s32[]{:T(128)}, ...), condition=%wide.region_5.6_spmd.clone, body=%wide.region_2.5_spmd.clone.sunk | while | flops 34611072 | bytes 2157681 | solution.py:189
  343.0 2.5 fusion.87
  346.2 73.3 %all-gather.24.cloned.1.call-done = bf16[1088,4352]{0,1:T(8,128)(2,1)} async-done(((bf16[1088,1088]{0,1:T(8,128)(2,1)}), bf16[1088,4352]{0,1:T(8,128)(2,1)}) %all-gather.24.cloned.1.call-update) | async-done | bytes 9469968 | tf_op jit(solution)/shard_map/all_gather | solution.py:80
  419.6 7.3 convolution_add_fusion
  426.9 8.2 fusion.88
  435.1 4.9 multiply_reduce_fusion
  442.6 133.4 %while.29 = (s32[]{:T(128)}, f32[17,128,64]{1,2,0:T(8,128)}, f32[17,1024,64]{1,2,0:T(8,128)}, f32[17,1024,64]{1,2,0:T(8,128)}, bf16[17,128,64]{2,1,0:T(8,128)(2,...) while((s32[]{:T(128)}, f32[17,128,64]{1,2,0:T(8,128)}, ...), condition=%wide.region_12.13_spmd.clone, body=%wide.region_10.12_spmd.clone.sunk | while | flops 85098368 | bytes 3944593 | solution.py:246
  576.7 3.0 fusion.71
  581.4 9.7 fusion.67
  593.0 35.7 %reduce-scatter.20.cloned.1.call-done = f32[128,1088]{0,1:T(8,128)} async-done(((f32[1024,1088]{0,1:T(8,128)}), f32[128,1088]{0,1:T(8,128)}) %reduce-scatter.20.cloned.1.call-update) | async-done | bytes 557072 | tf_op jit(solution)/shard_map/reduce_scatter | solution.py:252
  630.4 51.3 %reduce-scatter.22.cloned.1.call-done = f32[128,1088]{0,1:T(8,128)} async-done(((f32[1024,1088]{0,1:T(8,128)}), f32[128,1088]{0,1:T(8,128)}) %reduce-scatter.22.cloned.1.call-update) | async-done | bytes 557072 | tf_op jit(solution)/shard_map/reduce_scatter | solution.py:253
  684.5 8.5 fusion.65
  693.6 9.5 fusion.59
  703.2 37.2 %reduce-scatter.36.cloned.1.call-done = f32[136,1088]{1,0:T(8,128)} async-done(((f32[1088,1088]{1,0:T(8,128)}), f32[136,1088]{1,0:T(8,128)}) %reduce-scatter.36.cloned.1.call-update) | async-done | bytes 591888
  740.4 2.4 copy.110
  743.0 197.2 %reduce-scatter.28.cloned.1.call-done = f32[544,1088]{1,0:T(8,128)} async-done(((f32[4352,1088]{1,0:T(8,128)}), f32[544,1088]{1,0:T(8,128)}) %reduce-scatter.28.cloned.1.call-update) | async-done | bytes 2367504 | tf_op jit(solution)/shard_map/reduce_scatter | solution.py:93
  940.2 147.8 %reduce-scatter.24.cloned.1.call-done = f32[136,3264]{1,0:T(8,128)} async-done(((f32[1088,3264]{1,0:T(8,128)}), f32[136,3264]{1,0:T(8,128)}) %reduce-scatter.24.cloned.1.call-update) | async-done | bytes 1775632 | tf_op jit(solution)/shard_map/reduce_scatter | solution.py:90
  1088.0 3.4 copy.108
  1091.5 186.3 %reduce-scatter.26.cloned.1.call-done = f32[136,4352]{1,0:T(8,128)} async-done(((f32[1088,4352]{1,0:T(8,128)}), f32[136,4352]{1,0:T(8,128)}) %reduce-scatter.26.cloned.1.call-update) | async-done | bytes 2367504 | tf_op jit(solution)/shard_map/reduce_scatter | solution.py:92
  1277.8 5.0 copy.112
  1305.4 7.3 fusion.49
  1312.9 7.2 multiply_reduce_fusion.1
  1321.5 28.0 %all-reduce.2 = f32[1088,12]{0,1:T(8,128)} all-reduce(f32[1088,12]{0,1:T(8,128)} %concatenate.8), channel_id=12, replica_groups=mesh['dp'=4,'ctx'=8] {'ctx'}, use_global_device_ids=true, to_apply=%region_34.35.clone | all-reduce | flops 13056 | bytes 104448
  1350.9 17.5 %all-reduce.3 = f32[136,12]{0,1:T(8,128)} all-reduce(f32[136,12]{0,1:T(8,128)} %constant_dynamic-slice_fusion.2), channel_id=13, replica_groups=mesh['dp'=4,'ctx'=8] {'dp'}, use_global_device_ids=true, to_apply=%region_35.36.clone | all-reduce | flops 1632 | bytes 13056
  1376.0 11.3 all-reduce.6.cloned.1.call-done
  1387.3 3.9 multiply_subtract_fusion
  1391.2 2.4 copy.104
  1398.3 37.7 %reduce-scatter.30.cloned.1.call-done = f32[816,136]{1,0:T(8,128)} async-done(((f32[3264,136]{1,0:T(8,128)}), f32[816,136]{1,0:T(8,128)}) %reduce-scatter.30.cloned.1.call-update) | async-done | bytes 443920
  1437.4 2.7 multiply_subtract_fusion.2
  1440.1 53.6 %reduce-scatter.34.cloned.1.call-done = f32[1088,136]{1,0:T(8,128)} async-done(((f32[4352,136]{1,0:T(8,128)}), f32[1088,136]{1,0:T(8,128)}) %reduce-scatter.34.cloned.1.call-update) | async-done | bytes 591888
  1495.3 2.9 multiply_subtract_fusion.1
  (461 shorter events, 267.9 us)
Async XLA Ops:
  7.2 33.7 %all-gather.12.cloned.1.call-start = ((), (), s32[]{:S(2)}) async-start(), calls=%async_computation.10 | async-start | bytes 2193408 | tf_op jit(solution)/shard_map/all_gather | solution.py:71
  9.0 35.9 %copy-start.13 = (f32[544,272]{0,1:T(8,128)S(1)}, f32[544,272]{0,1:T(8,128)}, u32[]{:S(2)}) copy-start(f32[544,272]{0,1:T(8,128)} %param.28) | copy-start | bytes 1775620
  9.0 115.9 %all-gather.14.cloned.1.call-start = ((), (), s32[]{:S(2)}) async-start(), calls=%async_computation.11 | async-start | bytes 9400320 | tf_op jit(solution)/shard_map/all_gather | solution.py:78
  44.8 23.7 %copy-start.1 = (f32[1,128,1088]{1,2,0:T(8,128)S(1)}, f32[1,128,1088]{1,2,0:T(8,128)}, u32[]{:S(2)}) copy-start(f32[1,128,1088]{1,2,0:T(8,128)} %param.22) | copy-start | bytes 1671172
  44.9 123.4 %all-gather.26.cloned.1.call-start = ((), (), s32[]{:S(2)}) async-start(), calls=%async_computation.22 | async-start | bytes 3133440 | tf_op jit(solution)/shard_map/all_gather | solution.py:74
  45.7 156.0 %all-gather.22.cloned.1.call-start = ((), (), s32[]{:S(2)}) async-start(), calls=%async_computation.15 | async-start | bytes 2820096 | tf_op jit(solution)/shard_map/all_gather | solution.py:73
  46.8 187.8 %all-gather.16.cloned.1.call-start = ((), (), s32[]{:S(2)}) async-start(), calls=%async_computation.12 | async-start | bytes 2506752 | tf_op jit(solution)/shard_map/all_gather | solution.py:107
  69.4 61.0 %copy-start.32 = (f32[1088]{0:T(1024)}, f32[1088]{0:T(1024)S(1)}, u32[]{:S(2)}) copy-start(f32[1088]{0:T(1024)S(1)} %get-tuple-element.323) | copy-start | bytes 13060
  69.4 61.0 %copy-start.34 = (f32[1088]{0:T(1024)}, f32[1088]{0:T(1024)S(1)}, u32[]{:S(2)}) copy-start(f32[1088]{0:T(1024)S(1)} %get-tuple-element.322) | copy-start | bytes 13060
  69.4 61.1 %copy-start.47 = (f32[128]{0:T(128)}, f32[128]{0:T(128)S(1)}, u32[]{:S(2)}) copy-start(f32[128]{0:T(128)S(1)} %broadcast_multiply_fusion.6) | copy-start | bytes 1540
  69.5 60.9 %copy-start.51 = (f32[128]{0:T(128)}, f32[128]{0:T(128)S(1)}, u32[]{:S(2)}) copy-start(f32[128]{0:T(128)S(1)} %add_rsqrt_fusion.1) | copy-start | bytes 1540
  131.2 135.7 %all-gather.18.cloned.1.call-start = ((), (), s32[]{:S(2)}) async-start(), calls=%async_computation.13 | async-start | bytes 2506752 | tf_op jit(solution)/shard_map/all_gather | solution.py:108
  132.4 22.6 %copy-start.55 = (s32[8,2]{0,1:T(2,128)S(1)}, s32[8,2]{0,1:T(2,128)}, u32[]{:S(2)}) copy-start(s32[8,2]{0,1:T(2,128)} %param.24) | copy-start | bytes 196
  132.4 209.7 %all-gather.20.cloned.1.call-start = ((), (), s32[]{:S(2)}) async-start(), calls=%async_computation.14 | async-start | bytes 3133440 | tf_op jit(solution)/shard_map/all_gather | solution.py:79
  179.6 247.3 %all-to-all-start = ((bf16[4,4352,272]{1,2,0:T(8,128)(2,1)}), bf16[4,4352,272]{1,2,0:T(8,128)(2,1)}, u32[]{:S(2)}, u32[]{:S(2)}) async-start(bf16[4,4352,272]{1,2,0:T(8,128)(2,1)} %stack.36), calls=%async_computation | async-start | bytes 18939904 | tf_op jit(solution)/shard_map/all_to_all | solution.py:82
  185.4 234.2 %all-gather.24.cloned.1.call-start = ((), (), s32[]{:S(2)}) async-start(), calls=%async_computation.16 | async-start | bytes 12533760 | tf_op jit(solution)/shard_map/all_gather | solution.py:80
  206.9 421.7 %reduce-scatter.20.cloned.1.call-start = ((), (), s32[]{:S(2)}) async-start(), calls=%async_computation.17 | async-start | bytes 5013504 | tf_op jit(solution)/shard_map/reduce_scatter | solution.py:252
  272.2 70.7 %copy-start.37 = (f32[1088]{0:T(1024)S(1)}, f32[1088]{0:T(1024)}, u32[]{:S(2)}) copy-start(f32[1088]{0:T(1024)} %get-tuple-element.319) | copy-start | bytes 13060
  345.5 74.0 %copy-start.38 = (f32[128]{0:T(128)}, f32[128]{0:T(128)S(1)}, u32[]{:S(2)}) copy-start(f32[128]{0:T(128)S(1)} %broadcast_multiply_fusion.5) | copy-start | bytes 1540
  426.8 8.2 copy-start.3
  426.8 8.2 copy-start
  426.8 8.2 copy-start.31
  426.9 8.2 copy-start.39
  426.9 8.2 copy-start.41
  441.0 135.7 %copy-start.5 = (f32[128,1088]{0,1:T(8,128)}, f32[128,1088]{0,1:T(8,128)S(1)}, u32[]{:S(2)}) copy-start(f32[128,1088]{0,1:T(8,128)S(1)} %get-tuple-element.382) | copy-start | bytes 1671172
  576.1 105.6 %reduce-scatter.22.cloned.1.call-start = ((), (), s32[]{:S(2)}) async-start(), calls=%async_computation.18 | async-start | bytes 5013504 | tf_op jit(solution)/shard_map/reduce_scatter | solution.py:253
  576.7 163.8 %reduce-scatter.36.cloned.1.call-start = ((), (), s32[]{:S(2)}) async-start(), calls=%async_computation.27 | async-start | bytes 5640192
  579.8 360.4 %reduce-scatter.28.cloned.1.call-start = ((), (), s32[]{:S(2)}) async-start(), calls=%async_computation.21 | async-start | bytes 22560768 | tf_op jit(solution)/shard_map/reduce_scatter | solution.py:93
  591.1 93.4 %copy-start.48 = (f32[128]{0:T(128)S(1)}, f32[128]{0:T(128)}, u32[]{:S(2)}) copy-start(f32[128]{0:T(128)} %copy-done.47) | copy-start | bytes 1540
  591.1 496.9 %reduce-scatter.24.cloned.1.call-start = ((), (), s32[]{:S(2)}) async-start(), calls=%async_computation.19 | async-start | bytes 16293888 | tf_op jit(solution)/shard_map/reduce_scatter | solution.py:90
  693.0 584.8 %reduce-scatter.26.cloned.1.call-start = ((), (), s32[]{:S(2)}) async-start(), calls=%async_computation.20 | async-start | bytes 21307392 | tf_op jit(solution)/shard_map/reduce_scatter | solution.py:92
  703.2 669.6 %reduce-scatter.32.cloned.1.call-start = ((), (), s32[]{:S(2)}) async-start(), calls=%async_computation.24 | async-start | bytes 1392640
  742.9 644.4 %all-reduce.6.cloned.1.call-start = ((), (), s32[]{:S(2)}) async-start(), calls=%async_computation.26 | async-start | bytes 5013504
  940.2 495.8 %reduce-scatter.30.cloned.1.call-start = ((), (), s32[]{:S(2)}) async-start(), calls=%async_computation.23 | async-start | bytes 4177920
  1091.5 402.2 %reduce-scatter.34.cloned.1.call-start = ((), (), s32[]{:S(2)}) async-start(), calls=%async_computation.25 | async-start | bytes 5570560
  1282.8 11.5 copy-start.56
  1305.4 7.4 copy-start.27
  1305.4 7.4 copy-start.33
  1305.4 7.4 copy-start.49
  1305.4 7.4 copy-start.52
  1312.8 58.2 %copy-start.6 = (f32[128,1088]{0,1:T(8,128)S(1)}, f32[128,1088]{0,1:T(8,128)}, u32[]{:S(2)}) copy-start(f32[128,1088]{0,1:T(8,128)} %copy-done.5) | copy-start | bytes 1671172
  1321.5 65.9 %copy-start.9 = (f32[544,272]{1,0:T(8,128)S(1)}, f32[544,272]{1,0:T(8,128)}, u32[]{:S(2)}) copy-start(f32[544,272]{1,0:T(8,128)} %copy.103) | copy-start | bytes 1775620
  1321.5 65.9 %copy-start.10 = (f32[544,272]{1,0:T(8,128)S(1)}, f32[544,272]{1,0:T(8,128)}, u32[]{:S(2)}) copy-start(f32[544,272]{1,0:T(8,128)} %copy.100) | copy-start | bytes 1775620
  1373.9 17.3 %copy-start.29 = (f32[136,272]{1,0:T(8,128)}, f32[136,272]{1,0:T(8,128)S(1)}, u32[]{:S(2)}) copy-start(f32[136,272]{1,0:T(8,128)S(1)} %copy.111) | copy-start | bytes 443908
  1396.0 41.4 %copy-start.18 = (f32[136,816]{1,0:T(8,128)S(1)}, f32[136,816]{1,0:T(8,128)}, u32[]{:S(2)}) copy-start(f32[136,816]{1,0:T(8,128)} %param.25) | copy-start | bytes 1331716
  1437.4 57.9 %copy-start.17 = (f32[136,816]{1,0:T(8,128)}, f32[136,816]{1,0:T(8,128)S(1)}, u32[]{:S(2)}) copy-start(f32[136,816]{1,0:T(8,128)S(1)} %copy.109) | copy-start | bytes 1331716
  1437.4 57.9 %copy-start.15 = (f32[136,1088]{1,0:T(8,128)S(1)}, f32[136,1088]{1,0:T(8,128)}, u32[]{:S(2)}) copy-start(f32[136,1088]{1,0:T(8,128)} %param.27) | copy-start | bytes 1775620
  1437.4 57.9 %copy-start.30 = (f32[136,1088]{1,0:T(8,128)S(1)}, f32[136,1088]{1,0:T(8,128)}, u32[]{:S(2)}) copy-start(f32[136,1088]{1,0:T(8,128)} %param.32) | copy-start | bytes 1775620
  (28 other events, 122.3 us)
Sparse Core Ops, SparseCore 0:
  10.2 30.6 all-gather.11
  45.0 79.9 all-gather.13
  127.2 40.9 all-gather.25
  170.3 31.4 all-gather.21
  203.8 30.8 all-gather.15
  236.6 30.2 all-gather.17
  269.4 47.0 all-gather.19
  318.3 101.2 all-gather.23
  576.2 52.3 reduce-scatter.19
  630.8 50.8 reduce-scatter.21
  684.0 56.3 reduce-scatter.35
  742.7 197.4 reduce-scatter.27
  942.5 145.5 reduce-scatter.23
  1090.2 187.5 reduce-scatter.25
  1280.6 26.7 reduce-scatter.31
  1310.5 76.8 all-reduce.5
  1390.2 45.6 reduce-scatter.29
  1438.9 54.7 reduce-scatter.33
